TPU v7x, 32 devices: a whole 2x2x4 slice. The times are simulated.
32 devices in a mesh: section: 4 (over x, core), dp: 8 (over z, y).
Axes of the slice: x: 2, y: 2, z: 4, core: 2. Of those that a mesh axis runs over, the one named last changes fastest.
Arguments:
- latent_states: bfloat16 [4, 32, 96, 2048], P('section', 'dp'), may hold values from -8 to 8
- rescale_factor: float32 [2048], replicated, may hold values from 0.25 to 1.75
- embedding_matrix: bfloat16 [2048, 128], P('section'), may hold values from -0.125 to 0.125
- request_span: int32 [4, 32], replicated, may hold values from 8 to 32
- passage_span: int32 [4, 32], replicated, may hold values from 32 to 64
- matching_pair: int32 [4, 32], replicated, may hold values from 0 to 31, each once within a row
- steepness_pair: float32 [2], replicated, may hold values from 8 to 400
Outputs:
- grad_hidden: bfloat16 [4, 32, 96, 2048], P('section', 'dp')
- pair_loss: float32 [4, 32], P('section', 'dp')
Inputs may be any that keep to these rules, and one draw needn't show every extreme that they name: Each matching_pair[m] names every pair of the micro-batch once.
All inputs are finite; a program needn't handle non-finite values.
Results may differ from a plain program's by a relative error of at most 0.006.
The roundings to bfloat16 on the way count: a program that leaves them out, or rounds other values in their place, can miss the bound.
Values may be sent and summed in bfloat16 or wider, within the bound.
A program may use at most 64 MiB of HBM per device.

v0:
```python
import math
import jax
import jax.numpy as jnp
from jax import lax
from jax.sharding import PartitionSpec as P

QLEN = 32
DLEN = 64
EPSILON = 1e-06
OBJECTIVE_FACTOR = 1024.0
MASKED = -1e30


def head_forward(token_rows, rescale_factor, embedding_matrix):
    values = token_rows.astype(jnp.float32)
    inverse_rms = lax.rsqrt(jnp.mean(values * values, axis=-1, keepdims=True) + EPSILON)
    normed = (values * inverse_rms * rescale_factor).astype(jnp.bfloat16)
    projected = jnp.dot(normed, embedding_matrix, preferred_element_type=jnp.float32)
    inverse_length = lax.rsqrt(jnp.sum(projected * projected, axis=-1, keepdims=True) + EPSILON)
    vectors = (projected * inverse_length).astype(jnp.bfloat16)
    return (vectors, projected, inverse_length, inverse_rms)


def head_backward(
    token_rows,
    rescale_factor,
    embedding_matrix,
    projected,
    inverse_length,
    inverse_rms,
    grad_vectors,
):
    unit = projected * inverse_length
    along = jnp.sum(unit * grad_vectors, axis=-1, keepdims=True)
    grad_projected = (inverse_length * (grad_vectors - unit * along)).astype(jnp.bfloat16)
    grad_normed = lax.dot_general(
        grad_projected,
        embedding_matrix,
        (((1,), (1,)), ((), ())),
        preferred_element_type=jnp.float32,
    )
    values = token_rows.astype(jnp.float32)
    weighted = grad_normed * rescale_factor
    mean_term = jnp.mean(values * weighted, axis=-1, keepdims=True)
    grad_rows = (
        inverse_rms * weighted - values * (inverse_rms * inverse_rms * inverse_rms) * mean_term
    )
    return grad_rows.astype(jnp.bfloat16)


def pool_tokens(similarity, pooling_steepness, live):
    scaled = jnp.where(live[None], pooling_steepness * similarity, MASKED)
    highest = jnp.max(scaled, axis=2, keepdims=True)
    exponent = jnp.exp(scaled - highest)
    totals = jnp.sum(exponent, axis=2, keepdims=True)
    smooth = (highest[:, :, 0] + jnp.log(totals[:, :, 0])) / pooling_steepness
    return (smooth, exponent / totals)


def versus_term(relevance_matrix, matching_pair, logit_multiplier):
    unnormalized_odds = logit_multiplier * relevance_matrix
    highest = jnp.max(unnormalized_odds, axis=1, keepdims=True)
    log_total = highest[:, 0] + jnp.log(jnp.sum(jnp.exp(unnormalized_odds - highest), axis=1))
    columns = jnp.arange(relevance_matrix.shape[1], dtype=jnp.int32)
    correct_label = (columns[None, :] == matching_pair[:, None]).astype(jnp.float32)
    objective_value = log_total - jnp.sum(unnormalized_odds * correct_label, axis=1)
    probability_share = jnp.exp(unnormalized_odds - log_total[:, None])
    score_slope = OBJECTIVE_FACTOR * logit_multiplier * (probability_share - correct_label)
    return (objective_value, score_slope)


def query_weights(request_span, count):
    places = jnp.arange(count, dtype=jnp.int32)
    ones = jnp.where(places[None, :] < request_span[:, None], 1.0, 0.0).astype(jnp.float32)
    return ones / request_span[:, None].astype(jnp.float32)


def live_tokens(passage_span, count):
    places = jnp.arange(count, dtype=jnp.int32)
    return places[None, :] < passage_span[:, None]


def own_rows_pass(query_rows, own_weights, documents, live_all, pooling_steepness):
    pairs = own_weights.shape[0]
    features = query_rows.shape[1]
    total_pairs = documents.shape[0]
    group = math.gcd(total_pairs, max(1, 2048 // DLEN))
    blocks = total_pairs // group

    def block_similarity(start, count):
        docs_block = lax.dynamic_slice_in_dim(documents, start, count, 0).reshape(
            count * DLEN, features
        )
        live_block = lax.dynamic_slice_in_dim(live_all, start, count, 0)
        similarity = lax.dot_general(
            query_rows, docs_block, (((1,), (1,)), ((), ())), preferred_element_type=jnp.float32
        )
        return (similarity.reshape(pairs * QLEN, count, DLEN), live_block, docs_block)

    def forward_pass(index):
        similarity, live_block, _ = block_similarity(index * group, group)
        smooth, _ = pool_tokens(similarity, pooling_steepness, live_block)
        return jnp.sum(smooth.reshape(pairs, QLEN, group) * own_weights[:, :, None], axis=1)

    block_ids = jnp.arange(blocks, dtype=jnp.int32)
    relevance_matrix = lax.map(forward_pass, block_ids)
    relevance_matrix = jnp.transpose(relevance_matrix, (1, 0, 2)).reshape(pairs, total_pairs)
    return (relevance_matrix, block_similarity, group, block_ids)


def own_query_grads(
    query_rows, own_weights, score_slope, block_similarity, group, block_ids, pooling_steepness
):
    pairs = own_weights.shape[0]
    features = query_rows.shape[1]

    def gradient_block(start, count):
        similarity, live_block, docs_block = block_similarity(start, count)
        _, token_weight = pool_tokens(similarity, pooling_steepness, live_block)
        grad_block = lax.dynamic_slice_in_dim(score_slope, start, count, 1)
        coefficient = (own_weights[:, :, None] * grad_block[:, None, :]).reshape(
            pairs * QLEN, count
        )
        similarity_gradient = (coefficient[:, :, None] * token_weight).astype(jnp.bfloat16)
        return (similarity_gradient.reshape(pairs * QLEN, count * DLEN), docs_block)

    def query_step(carry, index):
        similarity_gradient, docs_block = gradient_block(index * group, group)
        return (
            carry + jnp.dot(similarity_gradient, docs_block, preferred_element_type=jnp.float32),
            None,
        )

    grad_queries, _ = lax.scan(
        query_step, jnp.zeros((pairs * QLEN, features), jnp.float32), block_ids
    )
    return (grad_queries, gradient_block)


def own_doc_pass(queries, doc_rows, weights_all, own_live, grad_columns, pooling_steepness):
    total_pairs = queries.shape[0]
    features = doc_rows.shape[1]
    pairs = own_live.shape[0]
    group = math.gcd(total_pairs, max(1, 1024 // QLEN))
    blocks = total_pairs // group

    def block_similarity(index):
        query_block = lax.dynamic_slice_in_dim(queries, index * group, group, 0).reshape(
            group * QLEN, features
        )
        similarity = lax.dot_general(
            query_block, doc_rows, (((1,), (1,)), ((), ())), preferred_element_type=jnp.float32
        )
        block_weight = lax.dynamic_slice_in_dim(weights_all, index * group, group, 0)
        return (similarity.reshape(group * QLEN, pairs, DLEN), block_weight, query_block)

    def backward(carry, index):
        similarity, block_weight, query_block = block_similarity(index)
        _, token_weight = pool_tokens(similarity, pooling_steepness, own_live)
        grad_block = lax.dynamic_slice_in_dim(grad_columns, index * group, group, 0)
        coefficient = (block_weight[:, :, None] * grad_block[:, None, :]).reshape(
            group * QLEN, pairs
        )
        similarity_gradient = (
            (coefficient[:, :, None] * token_weight)
            .astype(jnp.bfloat16)
            .reshape(group * QLEN, pairs * DLEN)
        )
        carry = carry + lax.dot_general(
            similarity_gradient,
            query_block,
            (((0,), (0,)), ((), ())),
            preferred_element_type=jnp.float32,
        )
        return (carry, None)

    block_ids = jnp.arange(blocks, dtype=jnp.int32)
    return (block_similarity, block_ids, group, backward)


def with_both(
    own_queries,
    own_docs,
    weights_all,
    live_all,
    selected_entry,
    first,
    pooling_steepness,
    logit_multiplier,
):
    pairs = own_queries.shape[0]
    features = own_queries.shape[2]
    queries, documents = (
        lax.all_gather(own_queries, "dp", axis=0, tiled=True),
        lax.all_gather(own_docs, "dp", axis=0, tiled=True),
    )
    query_rows = own_queries.reshape(pairs * QLEN, features)
    doc_rows = own_docs.reshape(pairs * DLEN, features)
    own_weights = lax.dynamic_slice_in_dim(weights_all, first, pairs, 0)
    own_live = lax.dynamic_slice_in_dim(live_all, first, pairs, 0)
    relevance_matrix, block_similarity, group, block_ids = own_rows_pass(
        query_rows, own_weights, documents, live_all, pooling_steepness
    )
    all_scores = lax.all_gather(relevance_matrix, "dp", axis=0, tiled=True)
    loss_all, grad_all = versus_term(all_scores, selected_entry, logit_multiplier)
    objective_value = lax.dynamic_slice_in_dim(loss_all, first, pairs, 0)
    grad_rows = lax.dynamic_slice_in_dim(grad_all, first, pairs, 0)
    grad_columns = lax.dynamic_slice_in_dim(grad_all, first, pairs, 1)
    grad_queries, _ = own_query_grads(
        query_rows, own_weights, grad_rows, block_similarity, group, block_ids, pooling_steepness
    )
    _, doc_block_ids, _, backward = own_doc_pass(
        queries, doc_rows, weights_all, own_live, grad_columns, pooling_steepness
    )
    grad_docs, _ = lax.scan(
        backward, jnp.zeros((pairs * DLEN, features), jnp.float32), doc_block_ids
    )
    return (
        grad_queries.reshape(pairs, QLEN, features),
        grad_docs.reshape(pairs, DLEN, features),
        objective_value,
    )


def local(
    latent_states,
    rescale_factor,
    embedding_matrix,
    request_span,
    passage_span,
    matching_pair,
    steepness_pair,
):
    full_proj = lax.all_gather(embedding_matrix, "section", axis=0, tiled=True)
    batch = lax.axis_index("section")
    pairs = latent_states.shape[1]
    length = latent_states.shape[2]
    width = latent_states.shape[3]
    first = lax.axis_index("dp") * pairs
    pooling_steepness = steepness_pair[0]
    logit_multiplier = steepness_pair[1]
    request_spans = lax.dynamic_index_in_dim(request_span, batch, 0, keepdims=False)
    passage_spans = lax.dynamic_index_in_dim(passage_span, batch, 0, keepdims=False)
    selected_entry = lax.dynamic_index_in_dim(matching_pair, batch, 0, keepdims=False)
    weights_all = query_weights(request_spans, QLEN)
    live_all = live_tokens(passage_spans, DLEN)
    flat_rows = latent_states.reshape(pairs * length, width)
    vectors, projected, inverse_length, inverse_rms = head_forward(
        flat_rows, rescale_factor, full_proj
    )
    vectors = vectors.reshape(pairs, length, -1)
    features = vectors.shape[2]
    own_queries = vectors[:, :QLEN]
    own_docs = vectors[:, QLEN:]
    grad_queries, grad_docs, objective_value = with_both(
        own_queries,
        own_docs,
        weights_all,
        live_all,
        selected_entry,
        first,
        pooling_steepness,
        logit_multiplier,
    )
    grad_vectors = jnp.concatenate([grad_queries, grad_docs], axis=1).reshape(
        pairs * length, features
    )
    grad_rows = head_backward(
        flat_rows, rescale_factor, full_proj, projected, inverse_length, inverse_rms, grad_vectors
    )
    return (grad_rows.reshape(1, pairs, length, width), objective_value[None, :])


def solution(mesh):
    return jax.shard_map(
        local,
        mesh=mesh,
        in_specs=(P("section", "dp", None, None), P(), P("section", None), P(), P(), P(), P()),
        out_specs=(P("section", "dp", None, None), P("section", "dp")),
        check_vma=False,
    )
```

profile of v0, /device:TPU:0, one launch (start us, length us, event | category | flops | bytes accessed | tf_op | source)
XLA Modules:
  0.0 135.8 jit_solution(408165753325786143)
XLA Ops:
  0.7 0.7 copy-done
  1.3 1.2 fusion.34
  2.5 1.3 fusion.36
  4.5 1.8 %fusion.2 = f32[4,96]{1,0:T(4,128)S(1)} fusion(bf16[1,4,96,2048]{3,2,1,0:T(8,128)(2,1)} %param.7), kind=kLoop, calls=%fused_computation.6 | loop fusion | flops 2358912 | bytes 1574400 | tf_op jit(solution)/shard_map/reduce_sum | solution.py:16
  7.7 0.7 div.65
  9.0 8.8 %all_gather.12 = bf16[2048,128]{1,0:T(8,128)(2,1)S(1)} all-gather(bf16[512,128]{1,0:T(8,128)(2,1)} %param.9), channel_id=1, replica_groups=mesh['section'=4,'dp'=8] {'section'}, dimensions={0}, use_global_device_ids=true | all-gather | bytes 655360 | tf_op jit(solution)/shard_map/all_gather | solution.py:234
  17.8 1.1 fusion.4
  19.0 0.7 multiply_reduce_fusion
  19.8 33.1 %all_gather.15 = bf16[32,32,128]{2,1,0:T(8,128)(2,1)} all-gather(bf16[4,32,128]{2,1,0:T(8,128)(2,1)S(1)} %slice.16), channel_id=1, replica_groups=mesh['section'=4,'dp'=8] {'dp'}, dimensions={0}, use_global_device_ids=true | all-gather | bytes 294912 | tf_op jit(solution)/shard_map/all_gather | solution.py:194
  52.9 31.2 %all_gather.13 = bf16[32,64,128]{2,1,0:T(8,128)(2,1)S(1)} all-gather(bf16[4,64,128]{2,1,0:T(8,128)(2,1)S(1)} %slice.17), channel_id=1, replica_groups=mesh['section'=4,'dp'=8] {'dp'}, dimensions={0}, use_global_device_ids=true | all-gather | bytes 589824 | tf_op jit(solution)/shard_map/all_gather | solution.py:195
  84.1 0.8 copy-done.2
  84.9 1.2 fusion.37
  86.3 1.3 add_divide_fusion
  87.6 0.8 div.62
  88.4 0.7 multiply_reduce_fusion.1
  89.1 0.8 copy.15
  89.9 26.1 %all-gather = f32[8,4,32]{2,1,0:T(4,128)S(1)} all-gather(f32[1,4,32]{2,1,0:T(4,128)S(1)} %bitcast.82), channel_id=1, replica_groups=mesh['section'=4,'dp'=8] {'dp'}, dimensions={0}, use_global_device_ids=true | all-gather | bytes 4608 | tf_op jit(solution)/shard_map/all_gather | solution.py:204
  116.0 0.7 fusion.33
  116.9 0.8 select_reduce_fusion
  117.6 0.7 subtract_multiply_fusion
  119.1 0.7 copy.16
  119.8 0.8 mul.254
  120.6 0.7 mul.255
  121.3 0.7 broadcast_multiply_fusion.2
  122.0 1.1 multiply_convert_fusion
  123.2 0.7 broadcast_multiply_fusion.1
  123.9 3.2 %fusion.17 = f32[4,64,128]{2,1,0:T(8,128)} fusion(bf16[1024,128,1]{1,0,2:T(8,128)(2,1)} %bitcast.79, f32[1024,4]{0,1:T(4,128)S(1)} %broadcast_multiply_fusion.1, f32[]{:T(128)} %bitcast.4, pred[4,64]{1,0:T(4,128)(4,1)} %constant_dynamic-slice_fusion, bf16[4,96,128]{2,1,0:T(8,128)(2,1)S(1)} %bitcast.77), kind=kOutput, calls=%fused_computation.24 | convolution fusion | flops 135798912 | bytes 738304 | tf_op jit(solution)/shard_map/while/body/eval_jaxpr/dot_general | solution.py:169
  127.1 2.5 %copy.17 = bf16[128,32,64]{2,1,0:T(8,128)(2,1)} copy(bf16[128,32,64]{0,2,1:T(8,128)(2,1)S(1)} %copy-done.4) | data formatting | bytes 1048576 | tf_op jit(solution)/shard_map/while/body/eval_jaxpr/convert_element_type | solution.py:124
  129.6 2.0 %dot_general.32 = bf16[4,32,2048]{2,1,0:T(8,128)(2,1)S(1)} reshape(bf16[128,32,64]{2,1,0:T(8,128)(2,1)} %copy.17) | data formatting | bytes 1048576 | tf_op jit(solution)/shard_map/while/body/eval_jaxpr/dot_general | solution.py:130
  132.0 0.9 pad_maximum_fusion
  133.3 0.7 fusion.8
  134.0 1.8 %fusion.7 = bf16[384,2048]{1,0:T(8,128)(2,1)} fusion(bf16[1,4,96,2048]{3,2,1,0:T(8,128)(2,1)S(1)} %copy-done.1, f32[384,2048]{1,0:T(8,128)S(1)} %get-tuple-element.78, f32[384]{0:T(512)S(1)} %broadcast_multiply_fusion.3, f32[384]{0:T(512)S(1)} %copy-done.6, f32[384]{0:T(512)S(1)} %rsqrt.23), kind=kLoop, calls=%fused_computation.11 | loop fusion | flops 4718592 | bytes 6296064 | tf_op jit(solution)/shard_map/convert_element_type | solution.py:48
  (38 shorter events, 4.1 us)
Async XLA Ops:
  0.6 0.7 copy-start
  0.6 17.2 %copy-start.1 = (bf16[1,4,96,2048]{3,2,1,0:T(8,128)(2,1)S(1)}, bf16[1,4,96,2048]{3,2,1,0:T(8,128)(2,1)}, u32[]{:S(2)}) copy-start(bf16[1,4,96,2048]{3,2,1,0:T(8,128)(2,1)} %param.7) | copy-start | bytes 4718596
  84.1 0.8 copy-start.2
  123.1 4.0 %copy-start.4 = (bf16[128,32,64]{0,2,1:T(8,128)(2,1)S(1)}, bf16[128,32,64]{0,2,1:T(8,128)(2,1)}, u32[]{:S(2)}) copy-start(bf16[128,32,64]{0,2,1:T(8,128)(2,1)} %multiply_convert_fusion) | copy-start | bytes 1572868
  123.9 7.7 %copy-start.3 = (bf16[32,64,128]{2,1,0:T(8,128)(2,1)S(1)}, bf16[32,64,128]{2,1,0:T(8,128)(2,1)}, u32[]{:S(2)}) copy-start(bf16[32,64,128]{2,1,0:T(8,128)(2,1)} %copy-done.2) | copy-start | bytes 1572868
  127.1 6.2 %copy-start.5 = (f32[2048]{0:T(1024)S(1)}, f32[2048]{0:T(1024)}, u32[]{:S(2)}) copy-start(f32[2048]{0:T(1024)} %param.8) | copy-start | bytes 24580
  132.9 1.1 copy-start.6
where the time goes:
time: 137 us; the launch traced here: 136 us
  blocking collectives  99.2 us (72%)
  other arithmetic  15 us (11%)
  local copies, waits for them, and re-layouts  14.1 us (10%)
  matrix products  6.05 us (4%)
  between operations  1.46 us (1%)
    all_gather x1, blocking collectives, with_both(): lax.all_gather(own_queries, 'dp', axis=0, tiled=True)  33.1 us
    all_gather x1, blocking collectives, with_both(): lax.all_gather(own_docs, 'dp', axis=0, tiled=True)  31.2 us
    all_gather x1, blocking collectives, with_both(): all_scores = lax.all_gather(relevance_matrix, 'dp', axis=0, tiled=True)  26.1 us
    all_gather x1, blocking collectives, local(): full_proj = lax.all_gather(embedding_matrix, 'section', axis=0, tiled=True)  8.84 us
    dot_general x1, matrix products, backward(): lax.dot_general(similarity_gradient, query_block, (((0,), (0,)), ((), ())...  3.16 us

commit v1 on v0

--- a/solution.py
+++ b/solution.py
@@ -231,7 +231,14 @@
     matching_pair,
     steepness_pair,
 ):
-    full_proj = lax.all_gather(embedding_matrix, "section", axis=0, tiled=True)
+    ring = [embedding_matrix]
+    for hop in range(3):
+        ring.append(lax.ppermute(ring[-1], "section", [(dev, (dev + 1) % 4) for dev in range(4)]))
+    full_proj = jnp.roll(
+        jnp.concatenate(ring[::-1], axis=0),
+        (lax.axis_index("section") + 1) * ring[0].shape[0],
+        axis=0,
+    )
     batch = lax.axis_index("section")
     pairs = latent_states.shape[1]
     length = latent_states.shape[2]

time: 137 us -> 121 us (0.88)
  local copies, waits for them, and re-layouts: 14.1 us -> 4.91 us
  blocking collectives: 99.2 us -> 91.4 us
  other arithmetic: 15 us -> 9.12 us
  waiting for transfers between devices: 0 us -> 5.11 us
  starting transfers between devices: 0 us -> 3 us
    all_gather x1 -> x0, blocking collectives: 8.84 us -> none  [local(): full_proj = lax.all_gather(embedding_matrix, 'section', axis=0, tiled=True)]
    ppermute x0 -> x3, waiting for transfers between devices: none -> 5.11 us  [local(): lax.ppermute(ring[-1], 'section', [(dev, (dev + 1) % 4) for dev in range(...]
    ppermute x0 -> x3, starting transfers between devices: none -> 3 us  [local(): lax.ppermute(ring[-1], 'section', [(dev, (dev + 1) % 4) for dev in range(...]
    mul x3, local copies, waits for them, and re-layouts: 2.12 us -> 0.27 us  [gradient_block(): own_weights[:, :, None] * grad_block[:, None, :]]
  transfers between devices with their start and end apart: 0 -> 3, of which waited for: 0 -> 3; matrix products, arithmetic and copies ran while one was open for 0% -> 4% of each run, Pallas kernels for 0% -> 0%
where the time goes in v1:
time: 121 us
  blocking collectives  91.4 us (76%)
  other arithmetic  9.12 us (8%)
  matrix products  5.4 us (4%)
  waiting for transfers between devices  5.11 us (4%)
  local copies, waits for them, and re-layouts  4.91 us (4%)
  starting transfers between devices  3 us (2%)
  between operations  1.61 us (1%)
    all_gather x1, blocking collectives, with_both(): lax.all_gather(own_queries, 'dp', axis=0, tiled=True)  34.1 us
    all_gather x1, blocking collectives, with_both(): lax.all_gather(own_docs, 'dp', axis=0, tiled=True)  31.2 us
    all_gather x1, blocking collectives, with_both(): all_scores = lax.all_gather(relevance_matrix, 'dp', axis=0, tiled=True)  26.1 us
    ppermute x3, waiting for transfers between devices, local(): lax.ppermute(ring[-1], 'section', [(dev, (dev + 1) % 4) for dev in range(...  5.11 us
    ppermute x3, starting transfers between devices, local(): lax.ppermute(ring[-1], 'section', [(dev, (dev + 1) % 4) for dev in range(...  3 us
    dot_general x1, matrix products, backward(): lax.dot_general(similarity_gradient, query_block, (((0,), (0,)), ((), ())...  2.54 us
  transfers between devices with their start and end apart: 3, of which 3 were waited for; matrix products, arithmetic and copies ran while one was open for 4% of the time, Pallas kernels for 0%

profile of v1, /device:TPU:0, one launch (start us, length us, event | category | flops | bytes accessed | tf_op | source)
XLA Modules:
  0.0 120.5 jit_solution(9145701686501613927)
XLA Ops:
  0.7 0.5 collective-permute-start
  1.2 1.8 %fusion.2 = f32[4,96]{1,0:T(4,128)S(1)} fusion(bf16[1,4,96,2048]{3,2,1,0:T(8,128)(2,1)} %param.7), kind=kLoop, calls=%fused_computation.6 | loop fusion | flops 2358912 | bytes 1574400 | tf_op jit(solution)/shard_map/reduce_sum | solution.py:16
  3.1 0.7 fusion.39
  3.9 1.8 %fusion.4 = bf16[384,2048]{1,0:T(8,128)(2,1)S(1)} fusion(bf16[1,4,96,2048]{3,2,1,0:T(8,128)(2,1)} %param.7, f32[2048]{0:T(1024)} %param.8, f32[384]{0:T(512)S(1)} %rsqrt.23), kind=kLoop, calls=%fused_computation.8 | loop fusion | flops 3145728 | bytes 3155456 | tf_op jit(solution)/shard_map/convert_element_type | solution.py:17
  5.8 0.2 collective-permute-done
  6.0 2.5 %collective-permute-start.1 = (bf16[512,128]{1,0:T(8,128)(2,1)S(1)}, bf16[512,128]{1,0:T(8,128)(2,1)S(1)}, u32[]{:S(2)}, u32[]{:S(2)}) collective-permute-start(bf16[512,128]{1,0:T(8,128)(2,1)S(1)} %collective-permute-done), channel_id=1, source_target_pairs={{0,8},{8,16},{16,24},{24,0},{1,9},{9,17},{17,25},{25,1},{2,10},{10... | collective-permute-start | bytes 393224 | tf_op jit(solution)/shard_map/ppermute | solution.py:236
  8.4 0.6 fusion.41
  9.0 1.4 %collective-permute-done.1 = bf16[512,128]{1,0:T(8,128)(2,1)S(1)} collective-permute-done((bf16[512,128]{1,0:T(8,128)(2,1)S(1)}, bf16[512,128]{1,0:T(8,128)(2,1)S(1)}, u32[]{:S(2)}, u32[]{:S(2)}) %collective-permute-start.1) | collective-permute-done | bytes 131104 | tf_op jit(solution)/shard_map/ppermute | solution.py:236
  11.3 3.5 %collective-permute-done.2 = bf16[512,128]{1,0:T(8,128)(2,1)S(1)} collective-permute-done((bf16[512,128]{1,0:T(8,128)(2,1)S(1)}, bf16[512,128]{1,0:T(8,128)(2,1)S(1)}, u32[]{:S(2)}, u32[]{:S(2)}) %collective-permute-start.2) | collective-permute-done | bytes 131104 | tf_op jit(solution)/shard_map/ppermute | solution.py:236
  15.0 0.7 multiply_reduce_fusion
  15.7 0.1 multiply_convert_fusion.1
  15.9 34.1 %all_gather.11 = bf16[32,32,128]{2,1,0:T(8,128)(2,1)} all-gather(bf16[4,32,128]{2,1,0:T(8,128)(2,1)S(1)} %slice.16), channel_id=1, replica_groups=mesh['section'=4,'dp'=8] {'dp'}, dimensions={0}, use_global_device_ids=true | all-gather | bytes 294912 | tf_op jit(solution)/shard_map/all_gather | solution.py:194
  50.0 31.2 %all_gather.9 = bf16[32,64,128]{2,1,0:T(8,128)(2,1)S(1)} all-gather(bf16[4,64,128]{2,1,0:T(8,128)(2,1)S(1)} %slice.17), channel_id=1, replica_groups=mesh['section'=4,'dp'=8] {'dp'}, dimensions={0}, use_global_device_ids=true | all-gather | bytes 589824 | tf_op jit(solution)/shard_map/all_gather | solution.py:195
  81.1 1.2 %fusion.42 = (f32[128,32]{0,1:T(8,128)S(1)}, f32[128,32,64]{0,2,1:T(8,128)S(1)}) fusion(bf16[128,128,1]{1,0,2:T(8,128)(2,1)S(1)} %bitcast.76, bf16[32,64,128]{2,1,0:T(8,128)(2,1)S(1)} %all_gather.9, f32[]{:T(128)} %bitcast.4, pred[32,64]{1,0:T(8,128)(4,1)S(1)} %iota_compare_fusion.1), kind=kOutput, calls=%fused_computation.87 | convolution fusion | flops 67891200 | bytes 1624068 | tf_op jit(solution)/shard_map/while/body/eval_jaxpr/dot_general | solution.py:95
  82.4 0.2 fusion.18
  82.6 0.7 add_divide_fusion
  83.3 0.1 multiply_reduce_fusion.1
  83.5 26.1 %all-gather = f32[8,4,32]{2,1,0:T(4,128)S(1)} all-gather(f32[1,4,32]{2,1,0:T(4,128)S(1)} %bitcast.80), channel_id=1, replica_groups=mesh['section'=4,'dp'=8] {'dp'}, dimensions={0}, use_global_device_ids=true | all-gather | bytes 4608 | tf_op jit(solution)/shard_map/all_gather | solution.py:204
  109.6 0.7 fusion.38
  110.5 0.2 select_reduce_fusion
  110.9 0.6 dynamic-slice_bitcast_fusion
  111.7 0.1 mul.259
  111.8 0.3 multiply_convert_fusion
  112.2 0.1 mul.265
  112.3 1.6 %copy.17 = bf16[128,32,64]{2,1,0:T(8,128)(2,1)S(1)} copy(bf16[128,32,64]{0,2,1:T(8,128)(2,1)S(1)} %multiply_convert_fusion) | data formatting | bytes 1048576 | tf_op jit(solution)/shard_map/while/body/eval_jaxpr/convert_element_type | solution.py:124
  113.9 0.8 dot_general.32
  114.7 0.3 fusion.47
  115.0 2.5 %fusion.17 = f32[4,64,128]{2,1,0:T(8,128)S(1)} fusion(bf16[1024,128,1]{1,0,2:T(8,128)(2,1)} %bitcast.77, f32[1024,4]{0,1:T(4,128)S(1)} %broadcast_multiply_fusion.1, f32[]{:T(128)} %bitcast.4, pred[4,64]{1,0:T(4,128)(4,1)S(1)} %constant_dynamic-slice_fusion, bf16[4,96,128]{2,1,0:T(8,128)(2,1)S(1)} %bitcast.75), kind=kOutput, calls=%fused_computation.24 | convolution fusion | flops 135798912 | bytes 738304 | tf_op jit(solution)/shard_map/while/body/eval_jaxpr/dot_general | solution.py:169
  117.6 0.2 fusion.23
  117.8 0.2 fusion.25
  118.0 0.7 fusion.8
  118.7 1.8 %fusion.7 = bf16[384,2048]{1,0:T(8,128)(2,1)} fusion(bf16[1,4,96,2048]{3,2,1,0:T(8,128)(2,1)S(1)} %copy-done.1, f32[384,2048]{1,0:T(8,128)S(1)} %get-tuple-element.78, f32[384]{0:T(512)S(1)} %broadcast_multiply_fusion.3, f32[384]{0:T(512)S(1)} %multiply_multiply_fusion, f32[384]{0:T(512)S(1)} %rsqrt.23), kind=kLoop, calls=%fused_computation.11 | loop fusion | flops 4718592 | bytes 6296064 | tf_op jit(solution)/shard_map/convert_element_type | solution.py:48
  (47 shorter events, 1.4 us)
Async XLA Ops:
  0.6 2.5 %copy-start = (s32[4,32]{1,0:T(4,128)S(1)}, s32[4,32]{1,0:T(4,128)}, u32[]{:S(2)}) copy-start(s32[4,32]{1,0:T(4,128)} %param.11) | copy-start | bytes 1540
  0.6 14.3 %copy-start.2 = (bf16[512,128]{1,0:T(8,128)(2,1)S(1)}, bf16[512,128]{1,0:T(8,128)(2,1)}, u32[]{:S(2)}) copy-start(bf16[512,128]{1,0:T(8,128)(2,1)} %param.9) | copy-start | bytes 393220
  0.7 7.8 %copy-start.4 = (f32[2]{0:T(128)S(1)}, f32[2]{0:T(128)}, u32[]{:S(2)}) copy-start(f32[2]{0:T(128)} %param.13) | copy-start | bytes 28
  0.7 5.3 %collective-permute-start = (bf16[512,128]{1,0:T(8,128)(2,1)}, bf16[512,128]{1,0:T(8,128)(2,1)S(1)}, u32[]{:S(2)}, u32[]{:S(2)}) collective-permute-start(bf16[512,128]{1,0:T(8,128)(2,1)} %param.9), channel_id=1, source_target_pairs={{0,8},{8,16},{16,24},{24,0},{1,9},{9,17},{17,25},{25,1},{2,10},{10... | collective-permute-start | bytes 393224 | tf_op jit(solution)/shard_map/ppermute | solution.py:236
  6.0 4.5 %collective-permute-start.1 = (bf16[512,128]{1,0:T(8,128)(2,1)S(1)}, bf16[512,128]{1,0:T(8,128)(2,1)S(1)}, u32[]{:S(2)}, u32[]{:S(2)}) collective-permute-start(bf16[512,128]{1,0:T(8,128)(2,1)S(1)} %collective-permute-done), channel_id=1, source_target_pairs={{0,8},{8,16},{16,24},{24,0},{1,9},{9,17},{17,25},{25,1},{2,10},{10... | collective-permute-start | bytes 393224 | tf_op jit(solution)/shard_map/ppermute | solution.py:236
  10.4 4.4 %collective-permute-start.2 = (bf16[512,128]{1,0:T(8,128)(2,1)S(1)}, bf16[512,128]{1,0:T(8,128)(2,1)S(1)}, u32[]{:S(2)}, u32[]{:S(2)}) collective-permute-start(bf16[512,128]{1,0:T(8,128)(2,1)S(1)} %collective-permute-done.1), channel_id=1, source_target_pairs={{0,8},{8,16},{16,24},{24,0},{1,9},{9,17},{17,25},{25,1},{2,10},{10... | collective-permute-start | bytes 393224 | tf_op jit(solution)/shard_map/ppermute | solution.py:236
  115.0 3.0 %copy-start.1 = (bf16[1,4,96,2048]{3,2,1,0:T(8,128)(2,1)S(1)}, bf16[1,4,96,2048]{3,2,1,0:T(8,128)(2,1)}, u32[]{:S(2)}) copy-start(bf16[1,4,96,2048]{3,2,1,0:T(8,128)(2,1)} %param.7) | copy-start | bytes 4718596
  115.0 3.0 %copy-start.3 = (f32[2048]{0:T(1024)S(1)}, f32[2048]{0:T(1024)}, u32[]{:S(2)}) copy-start(f32[2048]{0:T(1024)} %param.8) | copy-start | bytes 24580
